TPU v7x, 256 devices: a whole 4x4x8 slice. The times are simulated.
256 devices in a mesh: grp: 4 (over y), seq: 64 (over x, z, core).
Axes of the slice: x: 4, y: 4, z: 8, core: 2. Of those that a mesh axis runs over, the one named last changes fastest.
Arguments:
- queries: bfloat16 [32768, 1024], P(('grp', 'seq')), may hold values from -6 to 6
- keys: bfloat16 [32768, 1024], P(('grp', 'seq')), may hold values from -11 to 11
- values: bfloat16 [32768, 1024], P(('grp', 'seq')), may hold values from -6 to 6
- forget: float32 [32768, 8], P(('grp', 'seq')), may hold values from 0 to 0.5
- beta: float32 [32768, 8], P(('grp', 'seq')), may hold values from 0 to 1
- level_weights: float32 [9, 32768, 8], P(None, ('grp', 'seq')), may hold values from 0.25 to 2
Outputs:
- output: float32 [32768, 1024], P(('grp', 'seq'))
All inputs are finite; a program needn't handle non-finite values.
Results may differ from a plain program's by a relative error of at most 0.0003.
Values sent between devices are 32-bit elements; how exact they have to be, the bound alone decides.
No kernel may reach another device: no remote copies, remote signals or barrier semaphores. Data moves between devices by JAX's collectives and lax.ppermute only.
A program may use at most 64 MiB of HBM per device.

v0:
```python
import jax
import jax.numpy as jnp
from jax import lax
from jax.experimental import pallas as pl
from jax.experimental.pallas import tpu as pltpu
from jax.sharding import PartitionSpec as P

AXES = ("grp", "seq")
NY, NX, NZ, NC = 4, 4, 8, 2
HEADS = 8
D = 128
LEVELS = 8
F32 = jnp.float32
SQ = (D, D)
WIDE = (D, 2 * D)


BF16 = jnp.bfloat16


def halves(array):
    high = array.astype(BF16)
    return high, (array - high.astype(F32)).astype(BF16)


def mm_halves(left, right):
    n = right[0].shape[1]
    right = jnp.concatenate(right, 1)
    prod = jnp.dot(
        jnp.concatenate(left, 1),
        jnp.concatenate([right, right], 0),
        preferred_element_type=F32,
    )
    return prod[:, :n] + prod[:, n:]


def mm(left, right):
    return mm_halves(halves(left), halves(right))


def iotas(rows, cols):
    return (
        lax.broadcasted_iota(jnp.int32, (rows, cols), 0),
        lax.broadcasted_iota(jnp.int32, (rows, cols), 1),
    )


def unit_rows(array):
    return array * lax.rsqrt(jnp.sum(array * array, -1, keepdims=True) + 1e-06)


def place():
    seq = lax.axis_index("seq")
    return seq & 1, (seq >> 4) & 3, (seq >> 1) & 7, lax.axis_index("grp")


def head_span(h):
    return slice(h * D, (h + 1) * D)


def join(upper, lower):
    prod = mm(upper[:, :D], lower)
    return jnp.concatenate([prod[:, :D], prod[:, D:] + upper[:, D:]], 1)


def state_kernel(
    k_hbm, v_hbm, f_hbm, b_hbm, ab_ref, uw_ref, kt_ref, decay_ref,
    k_ref, v_ref, f_ref, b_ref, sems,
):
    copies = [
        pltpu.make_async_copy(source, target, sems.at[i])
        for i, (source, target) in enumerate(
            ((f_hbm, f_ref), (b_hbm, b_ref), (k_hbm, k_ref), (v_hbm, v_ref))
        )
    ]
    for copy in copies:
        copy.start()
    row, col = iotas(D, D)
    copies[0].wait()
    copies[1].wait()
    causal = row >= col
    eye = (row == col).astype(F32)
    total = jnp.dot(
        causal.astype(F32), f_ref[...].T,
        precision=lax.Precision.HIGHEST, preferred_element_type=F32,
    )
    decays = jnp.exp(-total)
    decay_ref[...] = decays
    strength = b_ref[...].T
    scaled = strength / decays
    heads = range(HEADS)
    copies[2].wait()
    ks = [unit_rows(k_ref[:, head_span(h)].astype(F32)) for h in heads]
    kts = [ks[h].T for h in heads]
    lowers = []
    for h in heads:
        kt_ref[h] = kts[h]
        cross = mm(ks[h], kts[h])
        lowers.append(jnp.where(row > col, cross * strength[:, h : h + 1], 0.0))

    def mask(j):
        same = (row >> (j + 1)) == (col >> (j + 1))
        return same & (((row >> j) & 1) == 1) & (((col >> j) & 1) == 0)

    inverse = [eye - jnp.where(mask(0), lowers[h], 0.0) for h in heads]
    parts = [halves(lowers[h]) for h in heads]
    for j in range(1, 7):
        pick = mask(j).astype(F32).astype(BF16)
        now = [halves(inverse[h]) for h in heads]
        half = [mm_halves(now[h], [part * pick for part in parts[h]]) for h in heads]
        inverse = [inverse[h] - mm_halves(halves(half[h]), now[h]) for h in heads]
    uws = []
    copies[3].wait()
    for h in heads:
        vh = v_ref[:, head_span(h)].astype(F32)
        right = jnp.concatenate(
            [strength[:, h : h + 1] * ks[h], scaled[:, h : h + 1] * vh], 1
        )
        uws.append(mm(inverse[h], right))
    for h in heads:
        uw_ref[h] = uws[h]
        final = decays[D - 1 : D, h : h + 1]
        prod = mm(kts[h], uws[h])
        ab_ref[h, :, :D] = final * (eye - prod[:, :D])
        ab_ref[h, :, D:] = final * prod[:, D:]


def read_kernel(q_ref, kt_ref, uw_ref, decay_ref, lw_ref, r_ref, in_ref):
    row, col = iotas(D, D)
    causal = row >= col
    decays = decay_ref[...]
    weights = lw_ref[0].T
    heads = range(HEADS)
    qs = [unit_rows(q_ref[:, head_span(h)].astype(F32)) for h in heads]
    scores = [jnp.where(causal, mm(qs[h], kt_ref[h]), 0.0) for h in heads]
    for h in heads:
        seen = mm(scores[h], uw_ref[h])
        decay = decays[:, h : h + 1]
        r_ref[h] = decay * (qs[h] - seen[:, :D])
        in_ref[:, head_span(h)] = decay * seen[:, D:] * weights[:, h : h + 1]


def pair_kernel(own_ref, peer_ref, x0_ref, x1_ref, x2_ref, x3_ref, x4_ref):
    core, _, z, _ = place()

    def emit(lower, upper, sign):
        for d, out in ((1, x1_ref), (2, x2_ref), (3, x3_ref)):
            h = (z + NZ + sign * d) & (NZ - 1)
            out[...] = join(upper[h], lower[h])
        h = (z + 4) & (NZ - 1)
        if sign > 0:
            x4_ref[...] = mm(upper[h][:, :D], lower[h][:, :D])
        else:
            x4_ref[...] = mm(upper[h][:, :D], lower[h][:, D:]) + upper[h][:, D:]
        x0_ref[...] = join(upper[z], lower[z])

    @pl.when(core == 0)
    def _():
        emit(own_ref, peer_ref, 1)

    @pl.when(core == 1)
    def _():
        emit(peer_ref, own_ref, -1)


def rows_kernel(peer_ref, r_ref, in_ref, lw_ref, rp_ref, acc_ref):
    core = place()[0]
    for level in range(1, LEVELS + 1):
        rp_ref[:, D + level - 1, :] = lw_ref[level]

    @pl.when(core == 0)
    def _():
        rp_ref[:, :D, :] = r_ref[...]
        acc_ref[...] = in_ref[...]

    @pl.when(core == 1)
    def _():
        weights = lw_ref[1].T
        for h in range(HEADS):
            moved = mm(r_ref[h], peer_ref[h])
            rp_ref[h, :D, :] = moved[:, :D]
            acc_ref[:, head_span(h)] = (
                in_ref[:, head_span(h)] + moved[:, D:] * weights[:, h : h + 1]
            )


def ring_kernel(
    x0_ref, y1_ref, y2_ref, y3_ref, y4_ref, p1_ref, p2_ref, p3_ref, p4_ref,
    even_ref, two_ref, four_ref, ab_ref, half_ref, one_ref,
):
    core, _, z, _ = place()
    back = lambda d: (z + NZ - d) & (NZ - 1)
    ahead = lambda d: (z + d) & (NZ - 1)
    one_ref[z] = x0_ref[...]
    across = ahead(4)

    @pl.when(core == 0)
    def _():
        for d, own, peer in ((1, y1_ref, p1_ref), (2, y2_ref, p2_ref), (3, y3_ref, p3_ref)):
            one_ref[back(d)] = own[...]
            one_ref[ahead(d)] = peer[...]
        one_ref[across, :, :D] = y4_ref[...]
        one_ref[across, :, D:] = p4_ref[...]

    @pl.when(core == 1)
    def _():
        for d, own, peer in ((1, y1_ref, p1_ref), (2, y2_ref, p2_ref), (3, y3_ref, p3_ref)):
            one_ref[ahead(d)] = own[...]
            one_ref[back(d)] = peer[...]
        one_ref[across, :, :D] = p4_ref[...]
        one_ref[across, :, D:] = y4_ref[...]

    two = [join(one_ref[c + 1], one_ref[c]) for c in range(0, NZ, 2)]
    for c in range(4):
        even_ref[c] = one_ref[2 * c]
    for c in range(2):
        two_ref[c] = two[2 * c]
    four = [join(two[c + 1], two[c]) for c in (0, 2)]
    four_ref[...] = four[0]
    whole = join(four[1], four[0])
    ab_ref[...] = whole
    half_ref[...] = jnp.where(core == 0, whole[:, :D], whole[:, D:])


def gather_runs(core, slot, own_ref, y1_ref, y2_ref, p1_ref, p2_ref, runs_ref):
    runs_ref[slot] = own_ref[...]
    back, ahead, across = (slot + 3) & 3, (slot + 1) & 3, (slot + 2) & 3

    @pl.when(core == 0)
    def _():
        runs_ref[back] = y1_ref[...]
        runs_ref[ahead] = p1_ref[...]
        runs_ref[across, :, :D] = y2_ref[...]
        runs_ref[across, :, D:] = p2_ref[...]

    @pl.when(core == 1)
    def _():
        runs_ref[ahead] = y1_ref[...]
        runs_ref[back] = p1_ref[...]
        runs_ref[across, :, :D] = p2_ref[...]
        runs_ref[across, :, D:] = y2_ref[...]


def x_kernel(
    own_ref, y1_ref, y2_ref, p1_ref, p2_ref,
    ab_ref, half_ref, prior_ref, g_ref, runs_ref,
):
    core, slot, _, _ = place()
    gather_runs(core, slot, own_ref, y1_ref, y2_ref, p1_ref, p2_ref, runs_ref)
    r0, r1, r2, r3 = (runs_ref[i] for i in range(4))
    low, high = join(r1, r0), join(r3, r2)
    whole = join(high, low)
    ab_ref[...] = whole
    half_ref[...] = jnp.where(core == 0, whole[:, :D], whole[:, D:])
    three = mm(r2[:, :D], low)
    row, col = iotas(D, D)
    eye = (row == col).astype(F32)
    zero = jnp.zeros(SQ, F32)
    prior = jnp.where(slot == 0, eye, r0[:, :D])
    prior = jnp.where(slot == 2, low[:, :D], prior)
    prior_ref[...] = jnp.where(slot == 3, three[:, :D], prior)
    g_ref[:, :D] = jnp.where(slot == 1, r0[:, D:], jnp.where(slot == 3, r2[:, D:], zero))
    g_ref[:, D:] = jnp.where(
        slot == 2, low[:, D:], jnp.where(slot == 3, three[:, D:], zero)
    )


def near_kernel(rp_ref, even_ref, two_ref, four_ref, g_ref, far_ref, moved_ref):
    third = mm(even_ref[1][:, :D], two_ref[0])
    seventh = mm(even_ref[3][:, :D], two_ref[1])
    fifth = mm(even_ref[2][:, :D], four_ref[...])
    sixth = mm(two_ref[1][:, :D], four_ref[...])
    last = mm(seventh[:, :D], four_ref[...])
    first = even_ref[0]
    quarter = two_ref[0]
    middle = four_ref[...]
    plans = [
        (None, []),
        (first[:, :D], [(1, first[:, D:])]),
        (quarter[:, :D], [(2, quarter[:, D:])]),
        (third[:, :D], [(1, even_ref[1][:, D:]), (2, third[:, D:])]),
        (middle[:, :D], [(3, middle[:, D:])]),
        (fifth[:, :D], [(1, even_ref[2][:, D:]), (3, fifth[:, D:])]),
        (sixth[:, :D], [(2, two_ref[1][:, D:]), (3, sixth[:, D:])]),
        (last[:, :D], [(1, even_ref[3][:, D:]), (2, seventh[:, D:]), (3, last[:, D:])]),
    ]
    moved, partial = [], []
    for c, (prior, levels) in enumerate(plans):
        rows = rp_ref[c, :D, :]
        weights = rp_ref[c, D:, :].T
        total = jnp.zeros(SQ, F32)
        if prior is None:
            moved.append(rows)
        else:
            prod = mm(rows, jnp.concatenate([prior] + [m for _, m in levels], 1))
            moved.append(prod[:, :D])
            for i, (level, _) in enumerate(levels):
                total = total + weights[:, level : level + 1] * prod[:, (i + 1) * D : (i + 2) * D]
        partial.append((total, weights))
    for c in range(NZ):
        total, weights = partial[c]
        prod = mm(moved[c], g_ref[...])
        far_ref[c] = total + weights[:, 4:5] * prod[:, :D] + weights[:, 5:6] * prod[:, D:]
        moved_ref[c, :, :D] = weights[:, 6:7] * moved[c]
        moved_ref[c, :, D:] = weights[:, 7:8] * moved[c]


def far_kernel(
    own_ref, y1_ref, y2_ref, p1_ref, p2_ref, prior_ref, near_ref, moved_ref,
    out_ref, runs_ref,
):
    core, _, _, slot = place()
    gather_runs(core, slot, own_ref, y1_ref, y2_ref, p1_ref, p2_ref, runs_ref)
    r0, r1, r2 = (runs_ref[i] for i in range(3))
    zero = jnp.zeros(SQ, F32)
    low = mm(r1[:, :D], r0[:, D:]) + r1[:, D:]
    three = mm(r2[:, :D], low)
    even = jnp.where(slot == 1, r0[:, D:], jnp.where(slot == 3, r2[:, D:], zero))
    pair = jnp.where(slot == 2, low, jnp.where(slot == 3, three, zero))
    mats = mm(prior_ref[...], jnp.concatenate([even, pair], 1))
    mats = jnp.concatenate([mats[:, :D], mats[:, D:]], 0)
    for c in range(NZ):
        out_ref[c] = near_ref[c] + mm(moved_ref[c], mats)


def add_kernel(acc_ref, far_ref, out_ref):
    for h in range(HEADS):
        out_ref[:, head_span(h)] = acc_ref[:, head_span(h)] + far_ref[h]


VMEM = pl.BlockSpec(memory_space=pltpu.VMEM)
HBM = pl.BlockSpec(memory_space=pltpu.HBM)


def call(kernel, outs, *args, scratch=(), products=1, space=VMEM, grant=16):
    sizes = [a.size * a.dtype.itemsize for a in args]
    return pl.pallas_call(
        kernel,
        out_shape=tuple(jax.ShapeDtypeStruct(s, F32) for s in outs),
        in_specs=[space] * len(args),
        out_specs=tuple(VMEM for _ in outs),
        scratch_shapes=scratch,
        cost_estimate=pl.CostEstimate(
            flops=products * 6 * D**3, bytes_accessed=sum(sizes), transcendentals=0
        ),
        compiler_params=pltpu.CompilerParams(vmem_limit_bytes=grant << 20),
    )(*args)


def send(block, move):
    pairs = []
    for i in range(NY * NX * NZ * NC):
        y, x, z, c = move(i >> 6, (i >> 4) & 3, (i >> 1) & 7, i & 1)
        pairs.append((i, ((y & 3) << 6) | ((x & 3) << 4) | ((z & 7) << 1) | c))
    return lax.ppermute(block, AXES, pairs)


def swap_core(block):
    return send(block, lambda y, x, z, c: (y, x, z, c ^ 1))


def over_z(block):
    groups = [
        [(x << 4) | (z << 1) | c for z in range(NZ)] for x in range(NX) for c in range(NC)
    ]
    return lax.all_to_all(block, "seq", 0, 0, axis_index_groups=groups, tiled=True)


def z_apart(block, d):
    return send(block, lambda y, x, z, c: (y, x, z + (d if c == 0 else -d), c))


def x_apart(block, d):
    return send(block, lambda y, x, z, c: (y, x + (d if c == 0 else -d), z, c))


def y_apart(block, d):
    return send(block, lambda y, x, z, c: (y + (d if c == 0 else -d), x, z, c))


def on_device(queries, keys, values, forget, beta, level_weights):
    weights = jnp.transpose(level_weights, (0, 2, 1))
    each = lambda n, shape: (n,) + shape
    ab, uw, kt, decays = call(
        state_kernel,
        [each(HEADS, WIDE), each(HEADS, WIDE), each(HEADS, SQ), (D, HEADS)],
        *(pltpu.with_memory_space_constraint(a, pltpu.HBM) for a in (keys, values, forget.T, beta.T)),
        products=150, space=HBM,
        scratch=[
            pltpu.VMEM((D, HEADS * D), jnp.bfloat16),
            pltpu.VMEM((D, HEADS * D), jnp.bfloat16),
            pltpu.VMEM((HEADS, D), F32),
            pltpu.VMEM((HEADS, D), F32),
            pltpu.SemaphoreType.DMA((4,)),
        ],
    )
    peer = swap_core(ab)
    reached, inside = call(
        read_kernel, [each(HEADS, SQ), (D, HEADS * D)],
        queries, kt, uw, decays, weights, products=24,
    )
    peer, reached, inside = lax.optimization_barrier((peer, reached, inside))
    x = call(
        pair_kernel, [WIDE, WIDE, WIDE, WIDE, SQ], ab, peer, products=9
    )
    y = [z_apart(x[d], d) for d in (4, 3, 2, 1)][::-1]
    rp, acc = call(
        rows_kernel, [(HEADS, D + LEVELS, D), (D, HEADS * D)],
        peer, reached, inside, weights, products=16,
    )
    *y, acc = lax.optimization_barrier((*y, acc))
    p = [swap_core(block) for block in y]
    one, two, four, ring, half = call(
        ring_kernel, [each(4, WIDE), each(2, WIDE), WIDE, WIDE, SQ],
        x[0], *y, *p, products=350, scratch=[pltpu.VMEM((NZ, D, 2 * D), F32)],
    )
    y1, y2 = x_apart(ring, 1), x_apart(half, 2)
    rows = over_z(rp)
    p1, p2 = swap_core(y1), swap_core(y2)
    runs = [pltpu.VMEM((4, D, 2 * D), F32)]
    plane, half, prior, gx = call(
        x_kernel, [WIDE, SQ, SQ, WIDE],
        ring, y1, y2, p1, p2, scratch=runs, products=8,
    )
    y1, y2 = y_apart(plane, 1), y_apart(half, 2)
    near, moved = call(
        near_kernel, [each(NZ, SQ), each(NZ, WIDE)], rows, one, two, four, gx, products=40
    )
    y2, near, moved = lax.optimization_barrier((y2, near, moved))
    p1, p2 = swap_core(y1), swap_core(y2)
    (far,) = call(
        far_kernel, [each(NZ, SQ)],
        plane, y1, y2, p1, p2, prior, near, moved,
        scratch=runs, products=20,
    )
    back = over_z(far)
    (out,) = call(add_kernel, [(D, HEADS * D)], acc, back)
    return out


def solution(mesh):
    spec = P(AXES, None)
    return jax.shard_map(
        on_device,
        mesh=mesh,
        in_specs=(spec, spec, spec, spec, spec, P(None, AXES, None)),
        out_specs=spec,
        check_vma=False,
    )
```

profile of v0, /device:TPU:1, one launch (start us, length us, event | category | flops | bytes accessed | tf_op | source)
XLA Modules:
  0.0 75.7 jit_solution(17677981165191283136)
XLA Ops:
  0.0 4.4 %shard_map.64 = (f32[8,128,256]{2,1,0:T(8,128)S(1)}, f32[8,128,256]{2,1,0:T(8,128)S(1)}, f32[8,128,128]{2,1,0:T(8,128)S(1)}, f32[128,8]{1,0:T(8,128)S(1)}) custom-call(bf16[128,1024]{1,0:T(8,128)(2,1)} %k_hbm.1, bf16[128,1024]{1,0:T(8,128)(2,1)} %v_hbm.1, f32[8,128]{1,0:T(8,128)} %bitcast.5, f32[8,128]{1,0:T(8,128)} %bitcast.6), custom_call_target="tpu_custom_call" | custom-call | flops 1887436800 | bytes 532480 | tf_op jit(solution)/shard_map/pallas_call | solution.py:337
  4.4 3.3 %collective-permute-start = (f32[8,128,256]{2,1,0:T(8,128)S(1)}, f32[8,128,256]{2,1,0:T(8,128)S(1)}, u32[]{:S(2)}, u32[]{:S(2)}) collective-permute-start(f32[8,128,256]{2,1,0:T(8,128)S(1)} %get-tuple-element.40.own_ref), channel_id=1, source_target_pairs={{0,1},{1,0},{2,3},{3,2},{4,5},{5,4},{6,7},{7,6},{8,9},{9,8},{10,11... | collective-permute-start | bytes 3145736 | tf_op jit(solution)/shard_map/ppermute | solution.py:355
  7.8 0.8 %shard_map.65 = (f32[8,128,128]{2,1,0:T(8,128)S(1)}, f32[128,1024]{1,0:T(8,128)S(1)}) custom-call(bf16[128,1024]{1,0:T(8,128)(2,1)S(1)} %copy-done, f32[8,128,128]{2,1,0:T(8,128)S(1)} %get-tuple-element.41.kt_ref, f32[8,128,256]{2,1,0:T(8,128)S(1)} %get-tuple-element.42.uw_ref, f32[128,8]{1,0:T(8,128)S(1)} %get-tuple-element.43.decay_ref, ...), custom_call_target="tpu_custom_call" | custom-call | flops 301989888 | bytes 1875968 | tf_op jit(solution)/shard_map/pallas_call | solution.py:337
  8.6 1.5 %collective-permute-done.peer_ref = f32[8,128,256]{2,1,0:T(8,128)S(1)} collective-permute-done((f32[8,128,256]{2,1,0:T(8,128)S(1)}, f32[8,128,256]{2,1,0:T(8,128)S(1)}, u32[]{:S(2)}, u32[]{:S(2)}) %collective-permute-start) | collective-permute-done | bytes 1048608 | tf_op jit(solution)/shard_map/ppermute | solution.py:355
  10.4 3.9 %collective-permute-start.1 = (f32[128,256]{1,0:T(8,128)S(1)}, f32[128,256]{1,0:T(8,128)S(1)}, u32[]{:S(2)}, u32[]{:S(2)}) collective-permute-start(f32[128,256]{1,0:T(8,128)S(1)} %get-tuple-element.47), channel_id=1, source_target_pairs={{0,2},{1,15},{2,4},{3,1},{4,6},{5,3},{6,8},{7,5},{8,10},{9,7},{10,... | collective-permute-start | bytes 393224 | tf_op jit(solution)/shard_map/ppermute | solution.py:355
  14.3 1.2 %collective-permute-start.2 = (f32[128,256]{1,0:T(8,128)S(1)}, f32[128,256]{1,0:T(8,128)S(1)}, u32[]{:S(2)}, u32[]{:S(2)}) collective-permute-start(f32[128,256]{1,0:T(8,128)S(1)} %get-tuple-element.48), channel_id=1, source_target_pairs={{0,4},{1,13},{2,6},{3,15},{4,8},{5,1},{6,10},{7,3},{8,12},{9,5},{1... | collective-permute-start | bytes 393224 | tf_op jit(solution)/shard_map/ppermute | solution.py:355
  15.9 4.5 %collective-permute-start.4 = (f32[128,128]{1,0:T(8,128)S(1)}, f32[128,128]{1,0:T(8,128)S(1)}, u32[]{:S(2)}, u32[]{:S(2)}) collective-permute-start(f32[128,128]{1,0:T(8,128)S(1)} %get-tuple-element.50), channel_id=1, source_target_pairs={{0,8},{1,9},{2,10},{3,11},{4,12},{5,13},{6,14},{7,15},{8,0},{9,1},... | collective-permute-start | bytes 196616 | tf_op jit(solution)/shard_map/ppermute | solution.py:355
  20.4 1.4 %shard_map.67 = (f32[8,136,128]{2,1,0:T(8,128)}, f32[128,1024]{1,0:T(8,128)S(1)}) custom-call(f32[8,128,256]{2,1,0:T(8,128)S(1)} %collective-permute-done.peer_ref, f32[8,128,128]{2,1,0:T(8,128)S(1)} %get-tuple-element.51.r_ref, f32[128,1024]{1,0:T(8,128)S(1)} %get-tuple-element.52.in_ref, f32[9,8,128]{2,1,0:T(8,128)S(1)} %bitcast.4), custom_call_target="tpu_custom_call" | custom-call | flops 201326592 | bytes 2134016 | tf_op jit(solution)/shard_map/pallas_call | solution.py:337
  21.8 3.5 %all-to-all-start = ((f32[8,136,128]{2,1,0:T(8,128)}), f32[8,136,128]{2,1,0:T(8,128)S(1)}, u32[]{:S(2)}, u32[]{:S(2)}) async-start(f32[8,136,128]{2,1,0:T(8,128)} %get-tuple-element.64), calls=%async_computation | async-start | bytes 1114112 | tf_op jit(solution)/shard_map/all_to_all | solution.py:366
  25.3 1.1 %collective-permute-done.4.y4_ref = f32[128,128]{1,0:T(8,128)S(1)} collective-permute-done((f32[128,128]{1,0:T(8,128)S(1)}, f32[128,128]{1,0:T(8,128)S(1)}, u32[]{:S(2)}, u32[]{:S(2)}) %collective-permute-start.4) | collective-permute-done | bytes 65568 | tf_op jit(solution)/shard_map/ppermute | solution.py:355
  26.4 2.5 %collective-permute-start.5 = (f32[128,256]{1,0:T(8,128)S(1)}, f32[128,256]{1,0:T(8,128)S(1)}, u32[]{:S(2)}, u32[]{:S(2)}) collective-permute-start(f32[128,256]{1,0:T(8,128)S(1)} %collective-permute-done.1.y1_ref), channel_id=1, source_target_pairs={{0,1},{1,0},{2,3},{3,2},{4,5},{5,4},{6,7},{7,6},{8,9},{9,8},{10,11... | collective-permute-start | bytes 393224 | tf_op jit(solution)/shard_map/ppermute | solution.py:355
  29.5 1.3 %collective-permute-done.8.p4_ref = f32[128,128]{1,0:T(8,128)S(1)} collective-permute-done((f32[128,128]{1,0:T(8,128)S(1)}, f32[128,128]{1,0:T(8,128)S(1)}, u32[]{:S(2)}, u32[]{:S(2)}) %collective-permute-start.8) | collective-permute-done | bytes 65568 | tf_op jit(solution)/shard_map/ppermute | solution.py:355
  31.5 2.7 %collective-permute-start.9 = (f32[128,256]{1,0:T(8,128)S(1)}, f32[128,256]{1,0:T(8,128)S(1)}, u32[]{:S(2)}, u32[]{:S(2)}) collective-permute-start(f32[128,256]{1,0:T(8,128)S(1)} %get-tuple-element.60.own_ref), channel_id=1, source_target_pairs={{0,16},{1,49},{2,18},{3,51},{4,20},{5,53},{6,22},{7,55},{8,24},{9,... | collective-permute-start | bytes 393224 | tf_op jit(solution)/shard_map/ppermute | solution.py:355
  34.8 2.8 %collective-permute-done.9.y1_ref = f32[128,256]{1,0:T(8,128)S(1)} collective-permute-done((f32[128,256]{1,0:T(8,128)S(1)}, f32[128,256]{1,0:T(8,128)S(1)}, u32[]{:S(2)}, u32[]{:S(2)}) %collective-permute-start.9) | collective-permute-done | bytes 131104 | tf_op jit(solution)/shard_map/ppermute | solution.py:355
  38.1 1.8 %collective-permute-done.10.y2_ref = f32[128,128]{1,0:T(8,128)S(1)} collective-permute-done((f32[128,128]{1,0:T(8,128)S(1)}, f32[128,128]{1,0:T(8,128)S(1)}, u32[]{:S(2)}, u32[]{:S(2)}) %collective-permute-start.10) | collective-permute-done | bytes 65568 | tf_op jit(solution)/shard_map/ppermute | solution.py:355
  40.5 0.9 %collective-permute-done.12.p2_ref = f32[128,128]{1,0:T(8,128)S(1)} collective-permute-done((f32[128,128]{1,0:T(8,128)S(1)}, f32[128,128]{1,0:T(8,128)S(1)}, u32[]{:S(2)}, u32[]{:S(2)}) %collective-permute-start.12) | collective-permute-done | bytes 65568 | tf_op jit(solution)/shard_map/ppermute | solution.py:355
  41.9 2.8 %collective-permute-start.13 = (f32[128,256]{1,0:T(8,128)S(1)}, f32[128,256]{1,0:T(8,128)S(1)}, u32[]{:S(2)}, u32[]{:S(2)}) collective-permute-start(f32[128,256]{1,0:T(8,128)S(1)} %get-tuple-element.62.own_ref), channel_id=1, source_target_pairs={{0,64},{1,193},{2,66},{3,195},{4,68},{5,197},{6,70},{7,199},{8,72}... | collective-permute-start | bytes 393224 | tf_op jit(solution)/shard_map/ppermute | solution.py:355
  45.1 3.0 %collective-permute-done.13.y1_ref = f32[128,256]{1,0:T(8,128)S(1)} collective-permute-done((f32[128,256]{1,0:T(8,128)S(1)}, f32[128,256]{1,0:T(8,128)S(1)}, u32[]{:S(2)}, u32[]{:S(2)}) %collective-permute-start.13) | collective-permute-done | bytes 131104 | tf_op jit(solution)/shard_map/ppermute | solution.py:355
  48.5 1.1 %shard_map.70 = (f32[8,128,128]{2,1,0:T(8,128)S(1)}, f32[8,128,256]{2,1,0:T(8,128)S(1)}) custom-call(f32[8,136,128]{2,1,0:T(8,128)S(1)} %all-to-all-done.rp_ref, f32[4,128,256]{2,1,0:T(8,128)S(1)} %get-tuple-element.65.even_ref, f32[2,128,256]{2,1,0:T(8,128)S(1)} %get-tuple-element.66.two_ref, f32[128,256]{1,0:T(8,128)S(1)} %get-tuple-element.67.four_ref, ...), custom_call_target="tpu_custom_call" | custom-call | flops 503316480 | bytes 1605632 | tf_op jit(solution)/shard_map/pallas_call | solution.py:337
  50.3 0.8 %collective-permute-start.16 = (f32[128,128]{1,0:T(8,128)S(1)}, f32[128,128]{1,0:T(8,128)S(1)}, u32[]{:S(2)}, u32[]{:S(2)}) collective-permute-start(f32[128,128]{1,0:T(8,128)S(1)} %collective-permute-done.14.y2_ref), channel_id=1, source_target_pairs={{0,1},{1,0},{2,3},{3,2},{4,5},{5,4},{6,7},{7,6},{8,9},{9,8},{10,11... | collective-permute-start | bytes 196616 | tf_op jit(solution)/shard_map/ppermute | solution.py:355
  51.2 0.9 %collective-permute-done.16.p2_ref = f32[128,128]{1,0:T(8,128)S(1)} collective-permute-done((f32[128,128]{1,0:T(8,128)S(1)}, f32[128,128]{1,0:T(8,128)S(1)}, u32[]{:S(2)}, u32[]{:S(2)}) %collective-permute-start.16) | collective-permute-done | bytes 65568 | tf_op jit(solution)/shard_map/ppermute | solution.py:355
  52.1 1.0 %shard_map.71 = f32[8,128,128]{2,1,0:T(8,128)S(1)} custom-call(f32[128,256]{1,0:T(8,128)S(1)} %get-tuple-element.62.own_ref, f32[128,256]{1,0:T(8,128)S(1)} %collective-permute-done.13.y1_ref, f32[128,128]{1,0:T(8,128)S(1)} %collective-permute-done.14.y2_ref, f32[128,256]{1,0:T(8,128)S(1)} %collective-permute-done.15.p1_ref, ...), custom_call_target="tpu_custom_call" | custom-call | flops 251658240 | bytes 2162688 | tf_op jit(solution)/shard_map/pallas_call | solution.py:337
  53.1 21.7 %all_to_all.10.far_ref = f32[8,128,128]{2,1,0:T(8,128)S(1)} all-to-all(f32[8,128,128]{2,1,0:T(8,128)S(1)} %shard_map.71), channel_id=1, replica_groups={{0,2,4,6,8,10,12,14},{1,3,5,7,9,11,13,15},{16,18,20,22,24,26,28,30},{17..., dimensions={0} | all-to-all | bytes 1048576 | tf_op jit(solution)/shard_map/all_to_all | solution.py:366
  74.8 0.8 %shard_map.72 = f32[128,1024]{1,0:T(8,128)} custom-call(f32[128,1024]{1,0:T(8,128)S(1)} %get-tuple-element.54.acc_ref, f32[8,128,128]{2,1,0:T(8,128)S(1)} %all_to_all.10.far_ref), custom_call_target="tpu_custom_call" | custom-call | flops 12582912 | bytes 1048576 | tf_op jit(solution)/shard_map/pallas_call | solution.py:337
  (26 shorter events, 5.8 us)
Async XLA Ops:
  0.0 7.8 %copy-start = (bf16[128,1024]{1,0:T(8,128)(2,1)S(1)}, bf16[128,1024]{1,0:T(8,128)(2,1)}, u32[]{:S(2)}) copy-start(bf16[128,1024]{1,0:T(8,128)(2,1)} %q_ref.1) | copy-start | bytes 786436
  0.0 7.8 %copy-start.1 = (f32[9,128,8]{1,2,0:T(8,128)S(1)}, f32[9,128,8]{1,2,0:T(8,128)}, u32[]{:S(2)}) copy-start(f32[9,128,8]{1,2,0:T(8,128)} %param.11) | copy-start | bytes 110596
  4.4 5.6 %collective-permute-start = (f32[8,128,256]{2,1,0:T(8,128)S(1)}, f32[8,128,256]{2,1,0:T(8,128)S(1)}, u32[]{:S(2)}, u32[]{:S(2)}) collective-permute-start(f32[8,128,256]{2,1,0:T(8,128)S(1)} %get-tuple-element.40.own_ref), channel_id=1, source_target_pairs={{0,1},{1,0},{2,3},{3,2},{4,5},{5,4},{6,7},{7,6},{8,9},{9,8},{10,11... | collective-permute-start | bytes 3145736 | tf_op jit(solution)/shard_map/ppermute | solution.py:355
  10.4 16.0 %collective-permute-start.1 = (f32[128,256]{1,0:T(8,128)S(1)}, f32[128,256]{1,0:T(8,128)S(1)}, u32[]{:S(2)}, u32[]{:S(2)}) collective-permute-start(f32[128,256]{1,0:T(8,128)S(1)} %get-tuple-element.47), channel_id=1, source_target_pairs={{0,2},{1,15},{2,4},{3,1},{4,6},{5,3},{6,8},{7,5},{8,10},{9,7},{10,... | collective-permute-start | bytes 393224 | tf_op jit(solution)/shard_map/ppermute | solution.py:355
  14.3 12.1 %collective-permute-start.2 = (f32[128,256]{1,0:T(8,128)S(1)}, f32[128,256]{1,0:T(8,128)S(1)}, u32[]{:S(2)}, u32[]{:S(2)}) collective-permute-start(f32[128,256]{1,0:T(8,128)S(1)} %get-tuple-element.48), channel_id=1, source_target_pairs={{0,4},{1,13},{2,6},{3,15},{4,8},{5,1},{6,10},{7,3},{8,12},{9,5},{1... | collective-permute-start | bytes 393224 | tf_op jit(solution)/shard_map/ppermute | solution.py:355
  15.5 10.9 %collective-permute-start.3 = (f32[128,256]{1,0:T(8,128)S(1)}, f32[128,256]{1,0:T(8,128)S(1)}, u32[]{:S(2)}, u32[]{:S(2)}) collective-permute-start(f32[128,256]{1,0:T(8,128)S(1)} %get-tuple-element.49), channel_id=1, source_target_pairs={{0,6},{1,11},{2,8},{3,13},{4,10},{5,15},{6,12},{7,1},{8,14},{9,3},... | collective-permute-start | bytes 393224 | tf_op jit(solution)/shard_map/ppermute | solution.py:355
  15.9 10.5 %collective-permute-start.4 = (f32[128,128]{1,0:T(8,128)S(1)}, f32[128,128]{1,0:T(8,128)S(1)}, u32[]{:S(2)}, u32[]{:S(2)}) collective-permute-start(f32[128,128]{1,0:T(8,128)S(1)} %get-tuple-element.50), channel_id=1, source_target_pairs={{0,8},{1,9},{2,10},{3,11},{4,12},{5,13},{6,14},{7,15},{8,0},{9,1},... | collective-permute-start | bytes 196616 | tf_op jit(solution)/shard_map/ppermute | solution.py:355
  21.8 26.8 %all-to-all-start = ((f32[8,136,128]{2,1,0:T(8,128)}), f32[8,136,128]{2,1,0:T(8,128)S(1)}, u32[]{:S(2)}, u32[]{:S(2)}) async-start(f32[8,136,128]{2,1,0:T(8,128)} %get-tuple-element.64), calls=%async_computation | async-start | bytes 1114112 | tf_op jit(solution)/shard_map/all_to_all | solution.py:366
  26.4 4.3 %collective-permute-start.5 = (f32[128,256]{1,0:T(8,128)S(1)}, f32[128,256]{1,0:T(8,128)S(1)}, u32[]{:S(2)}, u32[]{:S(2)}) collective-permute-start(f32[128,256]{1,0:T(8,128)S(1)} %collective-permute-done.1.y1_ref), channel_id=1, source_target_pairs={{0,1},{1,0},{2,3},{3,2},{4,5},{5,4},{6,7},{7,6},{8,9},{9,8},{10,11... | collective-permute-start | bytes 393224 | tf_op jit(solution)/shard_map/ppermute | solution.py:355
  28.9 1.8 %collective-permute-start.6 = (f32[128,256]{1,0:T(8,128)S(1)}, f32[128,256]{1,0:T(8,128)S(1)}, u32[]{:S(2)}, u32[]{:S(2)}) collective-permute-start(f32[128,256]{1,0:T(8,128)S(1)} %collective-permute-done.2.y2_ref), channel_id=1, source_target_pairs={{0,1},{1,0},{2,3},{3,2},{4,5},{5,4},{6,7},{7,6},{8,9},{9,8},{10,11... | collective-permute-start | bytes 393224 | tf_op jit(solution)/shard_map/ppermute | solution.py:355
  29.0 1.8 %collective-permute-start.7 = (f32[128,256]{1,0:T(8,128)S(1)}, f32[128,256]{1,0:T(8,128)S(1)}, u32[]{:S(2)}, u32[]{:S(2)}) collective-permute-start(f32[128,256]{1,0:T(8,128)S(1)} %collective-permute-done.3.y3_ref), channel_id=1, source_target_pairs={{0,1},{1,0},{2,3},{3,2},{4,5},{5,4},{6,7},{7,6},{8,9},{9,8},{10,11... | collective-permute-start | bytes 393224 | tf_op jit(solution)/shard_map/ppermute | solution.py:355
  29.5 1.3 %collective-permute-start.8 = (f32[128,128]{1,0:T(8,128)S(1)}, f32[128,128]{1,0:T(8,128)S(1)}, u32[]{:S(2)}, u32[]{:S(2)}) collective-permute-start(f32[128,128]{1,0:T(8,128)S(1)} %collective-permute-done.4.y4_ref), channel_id=1, source_target_pairs={{0,1},{1,0},{2,3},{3,2},{4,5},{5,4},{6,7},{7,6},{8,9},{9,8},{10,11... | collective-permute-start | bytes 196616 | tf_op jit(solution)/shard_map/ppermute | solution.py:355
  31.5 6.1 %collective-permute-start.9 = (f32[128,256]{1,0:T(8,128)S(1)}, f32[128,256]{1,0:T(8,128)S(1)}, u32[]{:S(2)}, u32[]{:S(2)}) collective-permute-start(f32[128,256]{1,0:T(8,128)S(1)} %get-tuple-element.60.own_ref), channel_id=1, source_target_pairs={{0,16},{1,49},{2,18},{3,51},{4,20},{5,53},{6,22},{7,55},{8,24},{9,... | collective-permute-start | bytes 393224 | tf_op jit(solution)/shard_map/ppermute | solution.py:355
  34.2 5.6 %collective-permute-start.10 = (f32[128,128]{1,0:T(8,128)S(1)}, f32[128,128]{1,0:T(8,128)S(1)}, u32[]{:S(2)}, u32[]{:S(2)}) collective-permute-start(f32[128,128]{1,0:T(8,128)S(1)} %get-tuple-element.61), channel_id=1, source_target_pairs={{0,32},{1,33},{2,34},{3,35},{4,36},{5,37},{6,38},{7,39},{8,40},{9,... | collective-permute-start | bytes 196616 | tf_op jit(solution)/shard_map/ppermute | solution.py:355
  37.6 3.9 %collective-permute-start.11 = (f32[128,256]{1,0:T(8,128)S(1)}, f32[128,256]{1,0:T(8,128)S(1)}, u32[]{:S(2)}, u32[]{:S(2)}) collective-permute-start(f32[128,256]{1,0:T(8,128)S(1)} %collective-permute-done.9.y1_ref), channel_id=1, source_target_pairs={{0,1},{1,0},{2,3},{3,2},{4,5},{5,4},{6,7},{7,6},{8,9},{9,8},{10,11... | collective-permute-start | bytes 393224 | tf_op jit(solution)/shard_map/ppermute | solution.py:355
  39.9 1.5 %collective-permute-start.12 = (f32[128,128]{1,0:T(8,128)S(1)}, f32[128,128]{1,0:T(8,128)S(1)}, u32[]{:S(2)}, u32[]{:S(2)}) collective-permute-start(f32[128,128]{1,0:T(8,128)S(1)} %collective-permute-done.10.y2_ref), channel_id=1, source_target_pairs={{0,1},{1,0},{2,3},{3,2},{4,5},{5,4},{6,7},{7,6},{8,9},{9,8},{10,11... | collective-permute-start | bytes 196616 | tf_op jit(solution)/shard_map/ppermute | solution.py:355
  41.9 6.1 %collective-permute-start.13 = (f32[128,256]{1,0:T(8,128)S(1)}, f32[128,256]{1,0:T(8,128)S(1)}, u32[]{:S(2)}, u32[]{:S(2)}) collective-permute-start(f32[128,256]{1,0:T(8,128)S(1)} %get-tuple-element.62.own_ref), channel_id=1, source_target_pairs={{0,64},{1,193},{2,66},{3,195},{4,68},{5,197},{6,70},{7,199},{8,72}... | collective-permute-start | bytes 393224 | tf_op jit(solution)/shard_map/ppermute | solution.py:355
  44.7 5.6 %collective-permute-start.14 = (f32[128,128]{1,0:T(8,128)S(1)}, f32[128,128]{1,0:T(8,128)S(1)}, u32[]{:S(2)}, u32[]{:S(2)}) collective-permute-start(f32[128,128]{1,0:T(8,128)S(1)} %get-tuple-element.63), channel_id=1, source_target_pairs={{0,128},{1,129},{2,130},{3,131},{4,132},{5,133},{6,134},{7,135},{8... | collective-permute-start | bytes 196616 | tf_op jit(solution)/shard_map/ppermute | solution.py:355
  48.1 3.1 %collective-permute-start.15 = (f32[128,256]{1,0:T(8,128)S(1)}, f32[128,256]{1,0:T(8,128)S(1)}, u32[]{:S(2)}, u32[]{:S(2)}) collective-permute-start(f32[128,256]{1,0:T(8,128)S(1)} %collective-permute-done.13.y1_ref), channel_id=1, source_target_pairs={{0,1},{1,0},{2,3},{3,2},{4,5},{5,4},{6,7},{7,6},{8,9},{9,8},{10,11... | collective-permute-start | bytes 393224 | tf_op jit(solution)/shard_map/ppermute | solution.py:355
  50.3 1.7 %collective-permute-start.16 = (f32[128,128]{1,0:T(8,128)S(1)}, f32[128,128]{1,0:T(8,128)S(1)}, u32[]{:S(2)}, u32[]{:S(2)}) collective-permute-start(f32[128,128]{1,0:T(8,128)S(1)} %collective-permute-done.14.y2_ref), channel_id=1, source_target_pairs={{0,1},{1,0},{2,3},{3,2},{4,5},{5,4},{6,7},{7,6},{8,9},{9,8},{10,11... | collective-permute-start | bytes 196616 | tf_op jit(solution)/shard_map/ppermute | solution.py:355
where the time goes:
time: 75.9 us; the launch traced here: 75.7 us
  starting transfers between devices  28.9 us (38%)
  blocking collectives  21.7 us (29%)
  waiting for transfers between devices  13.9 us (18%)
  Pallas kernels  11.2 us (15%)
    ppermute x17, starting transfers between devices, send(): return lax.ppermute(block, AXES, pairs)  25.3 us
    all_to_all x1, blocking collectives, over_z(): lax.all_to_all(block, 'seq', 0, 0, axis_index_groups=groups, tiled=True)  21.7 us
    ppermute x17, waiting for transfers between devices, send(): return lax.ppermute(block, AXES, pairs)  13.9 us
    pallas_call x9, Pallas kernels, call(): pl.pallas_call(kernel, out_shape=tuple((jax.ShapeDtypeStruct(s, F32) for...  11.2 us
    all_to_all x1, starting transfers between devices, over_z(): lax.all_to_all(block, 'seq', 0, 0, axis_index_groups=groups, tiled=True)  3.54 us
  transfers between devices with their start and end apart: 18, of which 9 were waited for; matrix products, arithmetic and copies ran while one was open for 0% of the time, Pallas kernels for 6%

commit v1 on v0

--- a/solution.py
+++ b/solution.py
@@ -265,7 +265,7 @@
     )
 
 
-def near_kernel(rp_ref, even_ref, two_ref, four_ref, g_ref, far_ref, moved_ref):
+def near_kernel(rp_ref, even_ref, two_ref, four_ref, g_ref, prior_ref, far_ref, moved_ref):
     third = mm(even_ref[1][:, :D], two_ref[0])
     seventh = mm(even_ref[3][:, :D], two_ref[1])
     fifth = mm(even_ref[2][:, :D], four_ref[...])
@@ -299,14 +299,15 @@
         partial.append((total, weights))
     for c in range(NZ):
         total, weights = partial[c]
-        prod = mm(moved[c], g_ref[...])
-        far_ref[c] = total + weights[:, 4:5] * prod[:, :D] + weights[:, 5:6] * prod[:, D:]
-        moved_ref[c, :, :D] = weights[:, 6:7] * moved[c]
-        moved_ref[c, :, D:] = weights[:, 7:8] * moved[c]
+        prod = mm(moved[c], jnp.concatenate([g_ref[...], prior_ref[...]], 1))
+        carried = prod[:, 2 * D :]
+        far_ref[c] = total + weights[:, 4:5] * prod[:, :D] + weights[:, 5:6] * prod[:, D : 2 * D]
+        moved_ref[c, :, :D] = weights[:, 6:7] * carried
+        moved_ref[c, :, D:] = weights[:, 7:8] * carried
 
 
 def far_kernel(
-    own_ref, y1_ref, y2_ref, p1_ref, p2_ref, prior_ref, near_ref, moved_ref,
+    own_ref, y1_ref, y2_ref, p1_ref, p2_ref, near_ref, moved_ref,
     out_ref, runs_ref,
 ):
     core, _, _, slot = place()
@@ -317,28 +318,35 @@
     three = mm(r2[:, :D], low)
     even = jnp.where(slot == 1, r0[:, D:], jnp.where(slot == 3, r2[:, D:], zero))
     pair = jnp.where(slot == 2, low, jnp.where(slot == 3, three, zero))
-    mats = mm(prior_ref[...], jnp.concatenate([even, pair], 1))
-    mats = jnp.concatenate([mats[:, :D], mats[:, D:]], 0)
+    mats = jnp.concatenate([even, pair], 0)
     for c in range(NZ):
         out_ref[c] = near_ref[c] + mm(moved_ref[c], mats)
 
 
-def add_kernel(acc_ref, far_ref, out_ref):
-    for h in range(HEADS):
-        out_ref[:, head_span(h)] = acc_ref[:, head_span(h)] + far_ref[h]
+def add_kernel(acc_ref, far_ref, out_hbm, out_ref, sems):
+    copies = []
+    for i in range(4):
+        rows = slice(32 * i, 32 * (i + 1))
+        for h in range(HEADS):
+            out_ref[rows, head_span(h)] = acc_ref[rows, head_span(h)] + far_ref[h, rows, :]
+        copy = pltpu.make_async_copy(out_ref.at[rows], out_hbm.at[rows], sems.at[i])
+        copy.start()
+        copies.append(copy)
+    for copy in copies:
+        copy.wait()
 
 
 VMEM = pl.BlockSpec(memory_space=pltpu.VMEM)
 HBM = pl.BlockSpec(memory_space=pltpu.HBM)
 
 
-def call(kernel, outs, *args, scratch=(), products=1, space=VMEM, grant=16):
+def call(kernel, outs, *args, scratch=(), products=1, space=VMEM, out_space=VMEM, grant=16):
     sizes = [a.size * a.dtype.itemsize for a in args]
     return pl.pallas_call(
         kernel,
         out_shape=tuple(jax.ShapeDtypeStruct(s, F32) for s in outs),
         in_specs=[space] * len(args),
-        out_specs=tuple(VMEM for _ in outs),
+        out_specs=tuple(out_space for _ in outs),
         scratch_shapes=scratch,
         cost_estimate=pl.CostEstimate(
             flops=products * 6 * D**3, bytes_accessed=sum(sizes), transcendentals=0
@@ -424,17 +432,20 @@
     )
     y1, y2 = y_apart(plane, 1), y_apart(half, 2)
     near, moved = call(
-        near_kernel, [each(NZ, SQ), each(NZ, WIDE)], rows, one, two, four, gx, products=40
+        near_kernel, [each(NZ, SQ), each(NZ, WIDE)], rows, one, two, four, gx, prior, products=40
     )
     y2, near, moved = lax.optimization_barrier((y2, near, moved))
     p1, p2 = swap_core(y1), swap_core(y2)
     (far,) = call(
         far_kernel, [each(NZ, SQ)],
-        plane, y1, y2, p1, p2, prior, near, moved,
+        plane, y1, y2, p1, p2, near, moved,
         scratch=runs, products=20,
     )
     back = over_z(far)
-    (out,) = call(add_kernel, [(D, HEADS * D)], acc, back)
+    (out,) = call(
+        add_kernel, [(D, HEADS * D)], acc, back, out_space=HBM,
+        scratch=[pltpu.VMEM((D, HEADS * D), F32), pltpu.SemaphoreType.DMA((4,))],
+    )
     return out
 
 

time: 75.9 us -> 75.8 us (level)
  no operation moved by 1% of the time
where the time goes in v1:
time: 75.8 us; the launch traced here: 75.6 us
  starting transfers between devices  28.9 us (38%)
  blocking collectives  21.6 us (28%)
  waiting for transfers between devices  13.7 us (18%)
  Pallas kernels  11 us (15%)
    ppermute x17, starting transfers between devices, send(): return lax.ppermute(block, AXES, pairs)  25.3 us
    all_to_all x1, blocking collectives, over_z(): lax.all_to_all(block, 'seq', 0, 0, axis_index_groups=groups, tiled=True)  21.6 us
    ppermute x17, waiting for transfers between devices, send(): return lax.ppermute(block, AXES, pairs)  13.7 us
    pallas_call x9, Pallas kernels, call(): pl.pallas_call(kernel, out_shape=tuple((jax.ShapeDtypeStruct(s, F32) for...  11 us
    all_to_all x1, starting transfers between devices, over_z(): lax.all_to_all(block, 'seq', 0, 0, axis_index_groups=groups, tiled=True)  3.54 us
  transfers between devices with their start and end apart: 18, of which 9 were waited for; matrix products, arithmetic and copies ran while one was open for 0% of the time, Pallas kernels for 6%

profile of v1, /device:TPU:1, one launch (start us, length us, event | category | flops | bytes accessed | tf_op | source)
XLA Modules:
  0.0 75.6 jit_solution(3401547639986391950)
XLA Ops:
  0.0 4.4 %shard_map.64 = (f32[8,128,256]{2,1,0:T(8,128)S(1)}, f32[8,128,256]{2,1,0:T(8,128)S(1)}, f32[8,128,128]{2,1,0:T(8,128)S(1)}, f32[128,8]{1,0:T(8,128)S(1)}) custom-call(bf16[128,1024]{1,0:T(8,128)(2,1)} %k_hbm.1, bf16[128,1024]{1,0:T(8,128)(2,1)} %v_hbm.1, f32[8,128]{1,0:T(8,128)} %bitcast.5, f32[8,128]{1,0:T(8,128)} %bitcast.6), custom_call_target="tpu_custom_call" | custom-call | flops 1887436800 | bytes 532480 | tf_op jit(solution)/shard_map/pallas_call | solution.py:345
  4.4 3.3 %collective-permute-start = (f32[8,128,256]{2,1,0:T(8,128)S(1)}, f32[8,128,256]{2,1,0:T(8,128)S(1)}, u32[]{:S(2)}, u32[]{:S(2)}) collective-permute-start(f32[8,128,256]{2,1,0:T(8,128)S(1)} %get-tuple-element.40.own_ref), channel_id=1, source_target_pairs={{0,1},{1,0},{2,3},{3,2},{4,5},{5,4},{6,7},{7,6},{8,9},{9,8},{10,11... | collective-permute-start | bytes 3145736 | tf_op jit(solution)/shard_map/ppermute | solution.py:363
  7.8 0.8 %shard_map.65 = (f32[8,128,128]{2,1,0:T(8,128)S(1)}, f32[128,1024]{1,0:T(8,128)S(1)}) custom-call(bf16[128,1024]{1,0:T(8,128)(2,1)S(1)} %copy-done, f32[8,128,128]{2,1,0:T(8,128)S(1)} %get-tuple-element.41.kt_ref, f32[8,128,256]{2,1,0:T(8,128)S(1)} %get-tuple-element.42.uw_ref, f32[128,8]{1,0:T(8,128)S(1)} %get-tuple-element.43.decay_ref, ...), custom_call_target="tpu_custom_call" | custom-call | flops 301989888 | bytes 1875968 | tf_op jit(solution)/shard_map/pallas_call | solution.py:345
  8.6 1.5 %collective-permute-done.peer_ref = f32[8,128,256]{2,1,0:T(8,128)S(1)} collective-permute-done((f32[8,128,256]{2,1,0:T(8,128)S(1)}, f32[8,128,256]{2,1,0:T(8,128)S(1)}, u32[]{:S(2)}, u32[]{:S(2)}) %collective-permute-start) | collective-permute-done | bytes 1048608 | tf_op jit(solution)/shard_map/ppermute | solution.py:363
  10.4 3.9 %collective-permute-start.1 = (f32[128,256]{1,0:T(8,128)S(1)}, f32[128,256]{1,0:T(8,128)S(1)}, u32[]{:S(2)}, u32[]{:S(2)}) collective-permute-start(f32[128,256]{1,0:T(8,128)S(1)} %get-tuple-element.47), channel_id=1, source_target_pairs={{0,2},{1,15},{2,4},{3,1},{4,6},{5,3},{6,8},{7,5},{8,10},{9,7},{10,... | collective-permute-start | bytes 393224 | tf_op jit(solution)/shard_map/ppermute | solution.py:363
  14.3 1.2 %collective-permute-start.2 = (f32[128,256]{1,0:T(8,128)S(1)}, f32[128,256]{1,0:T(8,128)S(1)}, u32[]{:S(2)}, u32[]{:S(2)}) collective-permute-start(f32[128,256]{1,0:T(8,128)S(1)} %get-tuple-element.48), channel_id=1, source_target_pairs={{0,4},{1,13},{2,6},{3,15},{4,8},{5,1},{6,10},{7,3},{8,12},{9,5},{1... | collective-permute-start | bytes 393224 | tf_op jit(solution)/shard_map/ppermute | solution.py:363
  15.9 4.5 %collective-permute-start.4 = (f32[128,128]{1,0:T(8,128)S(1)}, f32[128,128]{1,0:T(8,128)S(1)}, u32[]{:S(2)}, u32[]{:S(2)}) collective-permute-start(f32[128,128]{1,0:T(8,128)S(1)} %get-tuple-element.50), channel_id=1, source_target_pairs={{0,8},{1,9},{2,10},{3,11},{4,12},{5,13},{6,14},{7,15},{8,0},{9,1},... | collective-permute-start | bytes 196616 | tf_op jit(solution)/shard_map/ppermute | solution.py:363
  20.4 1.4 %shard_map.67 = (f32[8,136,128]{2,1,0:T(8,128)}, f32[128,1024]{1,0:T(8,128)S(1)}) custom-call(f32[8,128,256]{2,1,0:T(8,128)S(1)} %collective-permute-done.peer_ref, f32[8,128,128]{2,1,0:T(8,128)S(1)} %get-tuple-element.51.r_ref, f32[128,1024]{1,0:T(8,128)S(1)} %get-tuple-element.52.in_ref, f32[9,8,128]{2,1,0:T(8,128)S(1)} %bitcast.4), custom_call_target="tpu_custom_call" | custom-call | flops 201326592 | bytes 2134016 | tf_op jit(solution)/shard_map/pallas_call | solution.py:345
  21.8 3.5 %all-to-all-start = ((f32[8,136,128]{2,1,0:T(8,128)}), f32[8,136,128]{2,1,0:T(8,128)S(1)}, u32[]{:S(2)}, u32[]{:S(2)}) async-start(f32[8,136,128]{2,1,0:T(8,128)} %get-tuple-element.64), calls=%async_computation | async-start | bytes 1114112 | tf_op jit(solution)/shard_map/all_to_all | solution.py:374
  25.3 1.1 %collective-permute-done.4.y4_ref = f32[128,128]{1,0:T(8,128)S(1)} collective-permute-done((f32[128,128]{1,0:T(8,128)S(1)}, f32[128,128]{1,0:T(8,128)S(1)}, u32[]{:S(2)}, u32[]{:S(2)}) %collective-permute-start.4) | collective-permute-done | bytes 65568 | tf_op jit(solution)/shard_map/ppermute | solution.py:363
  26.4 2.5 %collective-permute-start.5 = (f32[128,256]{1,0:T(8,128)S(1)}, f32[128,256]{1,0:T(8,128)S(1)}, u32[]{:S(2)}, u32[]{:S(2)}) collective-permute-start(f32[128,256]{1,0:T(8,128)S(1)} %collective-permute-done.1.y1_ref), channel_id=1, source_target_pairs={{0,1},{1,0},{2,3},{3,2},{4,5},{5,4},{6,7},{7,6},{8,9},{9,8},{10,11... | collective-permute-start | bytes 393224 | tf_op jit(solution)/shard_map/ppermute | solution.py:363
  29.5 1.3 %collective-permute-done.8.p4_ref = f32[128,128]{1,0:T(8,128)S(1)} collective-permute-done((f32[128,128]{1,0:T(8,128)S(1)}, f32[128,128]{1,0:T(8,128)S(1)}, u32[]{:S(2)}, u32[]{:S(2)}) %collective-permute-start.8) | collective-permute-done | bytes 65568 | tf_op jit(solution)/shard_map/ppermute | solution.py:363
  31.5 2.7 %collective-permute-start.9 = (f32[128,256]{1,0:T(8,128)S(1)}, f32[128,256]{1,0:T(8,128)S(1)}, u32[]{:S(2)}, u32[]{:S(2)}) collective-permute-start(f32[128,256]{1,0:T(8,128)S(1)} %get-tuple-element.60.own_ref), channel_id=1, source_target_pairs={{0,16},{1,49},{2,18},{3,51},{4,20},{5,53},{6,22},{7,55},{8,24},{9,... | collective-permute-start | bytes 393224 | tf_op jit(solution)/shard_map/ppermute | solution.py:363
  34.8 2.8 %collective-permute-done.9.y1_ref = f32[128,256]{1,0:T(8,128)S(1)} collective-permute-done((f32[128,256]{1,0:T(8,128)S(1)}, f32[128,256]{1,0:T(8,128)S(1)}, u32[]{:S(2)}, u32[]{:S(2)}) %collective-permute-start.9) | collective-permute-done | bytes 131104 | tf_op jit(solution)/shard_map/ppermute | solution.py:363
  38.1 1.8 %collective-permute-done.10.y2_ref = f32[128,128]{1,0:T(8,128)S(1)} collective-permute-done((f32[128,128]{1,0:T(8,128)S(1)}, f32[128,128]{1,0:T(8,128)S(1)}, u32[]{:S(2)}, u32[]{:S(2)}) %collective-permute-start.10) | collective-permute-done | bytes 65568 | tf_op jit(solution)/shard_map/ppermute | solution.py:363
  40.5 0.9 %collective-permute-done.12.p2_ref = f32[128,128]{1,0:T(8,128)S(1)} collective-permute-done((f32[128,128]{1,0:T(8,128)S(1)}, f32[128,128]{1,0:T(8,128)S(1)}, u32[]{:S(2)}, u32[]{:S(2)}) %collective-permute-start.12) | collective-permute-done | bytes 65568 | tf_op jit(solution)/shard_map/ppermute | solution.py:363
  41.9 2.8 %collective-permute-start.13 = (f32[128,256]{1,0:T(8,128)S(1)}, f32[128,256]{1,0:T(8,128)S(1)}, u32[]{:S(2)}, u32[]{:S(2)}) collective-permute-start(f32[128,256]{1,0:T(8,128)S(1)} %get-tuple-element.62.own_ref), channel_id=1, source_target_pairs={{0,64},{1,193},{2,66},{3,195},{4,68},{5,197},{6,70},{7,199},{8,72}... | collective-permute-start | bytes 393224 | tf_op jit(solution)/shard_map/ppermute | solution.py:363
  45.1 3.0 %collective-permute-done.13.y1_ref = f32[128,256]{1,0:T(8,128)S(1)} collective-permute-done((f32[128,256]{1,0:T(8,128)S(1)}, f32[128,256]{1,0:T(8,128)S(1)}, u32[]{:S(2)}, u32[]{:S(2)}) %collective-permute-start.13) | collective-permute-done | bytes 131104 | tf_op jit(solution)/shard_map/ppermute | solution.py:363
  48.5 1.2 %shard_map.70 = (f32[8,128,128]{2,1,0:T(8,128)S(1)}, f32[8,128,256]{2,1,0:T(8,128)S(1)}) custom-call(f32[8,136,128]{2,1,0:T(8,128)S(1)} %all-to-all-done.rp_ref, f32[4,128,256]{2,1,0:T(8,128)S(1)} %get-tuple-element.65.even_ref, f32[2,128,256]{2,1,0:T(8,128)S(1)} %get-tuple-element.66.two_ref, f32[128,256]{1,0:T(8,128)S(1)} %get-tuple-element.67.four_ref, ...), custom_call_target="tpu_custom_call" | custom-call | flops 503316480 | bytes 1671168 | tf_op jit(solution)/shard_map/pallas_call | solution.py:345
  50.3 0.8 %collective-permute-start.16 = (f32[128,128]{1,0:T(8,128)S(1)}, f32[128,128]{1,0:T(8,128)S(1)}, u32[]{:S(2)}, u32[]{:S(2)}) collective-permute-start(f32[128,128]{1,0:T(8,128)S(1)} %collective-permute-done.14.y2_ref), channel_id=1, source_target_pairs={{0,1},{1,0},{2,3},{3,2},{4,5},{5,4},{6,7},{7,6},{8,9},{9,8},{10,11... | collective-permute-start | bytes 196616 | tf_op jit(solution)/shard_map/ppermute | solution.py:363
  51.2 0.9 %collective-permute-done.16.p2_ref = f32[128,128]{1,0:T(8,128)S(1)} collective-permute-done((f32[128,128]{1,0:T(8,128)S(1)}, f32[128,128]{1,0:T(8,128)S(1)}, u32[]{:S(2)}, u32[]{:S(2)}) %collective-permute-start.16) | collective-permute-done | bytes 65568 | tf_op jit(solution)/shard_map/ppermute | solution.py:363
  52.1 0.8 %shard_map.71 = f32[8,128,128]{2,1,0:T(8,128)S(1)} custom-call(f32[128,256]{1,0:T(8,128)S(1)} %get-tuple-element.62.own_ref, f32[128,256]{1,0:T(8,128)S(1)} %collective-permute-done.13.y1_ref, f32[128,128]{1,0:T(8,128)S(1)} %collective-permute-done.14.y2_ref, f32[128,256]{1,0:T(8,128)S(1)} %collective-permute-done.15.p1_ref, ...), custom_call_target="tpu_custom_call" | custom-call | flops 251658240 | bytes 2097152 | tf_op jit(solution)/shard_map/pallas_call | solution.py:345
  52.9 21.6 %all_to_all.10.far_ref = f32[8,128,128]{2,1,0:T(8,128)S(1)} all-to-all(f32[8,128,128]{2,1,0:T(8,128)S(1)} %shard_map.71), channel_id=1, replica_groups={{0,2,4,6,8,10,12,14},{1,3,5,7,9,11,13,15},{16,18,20,22,24,26,28,30},{17..., dimensions={0} | all-to-all | bytes 1048576 | tf_op jit(solution)/shard_map/all_to_all | solution.py:374
  74.6 0.8 %shard_map.72 = f32[128,1024]{1,0:T(8,128)} custom-call(f32[128,1024]{1,0:T(8,128)S(1)} %get-tuple-element.54.acc_ref, f32[8,128,128]{2,1,0:T(8,128)S(1)} %all_to_all.10.far_ref), custom_call_target="tpu_custom_call" | custom-call | flops 12582912 | bytes 1048576 | tf_op jit(solution)/shard_map/pallas_call | solution.py:345
  (26 shorter events, 5.7 us)
Async XLA Ops:
  0.0 7.8 %copy-start = (bf16[128,1024]{1,0:T(8,128)(2,1)S(1)}, bf16[128,1024]{1,0:T(8,128)(2,1)}, u32[]{:S(2)}) copy-start(bf16[128,1024]{1,0:T(8,128)(2,1)} %q_ref.1) | copy-start | bytes 786436
  0.0 7.8 %copy-start.1 = (f32[9,128,8]{1,2,0:T(8,128)S(1)}, f32[9,128,8]{1,2,0:T(8,128)}, u32[]{:S(2)}) copy-start(f32[9,128,8]{1,2,0:T(8,128)} %param.11) | copy-start | bytes 110596
  4.4 5.6 %collective-permute-start = (f32[8,128,256]{2,1,0:T(8,128)S(1)}, f32[8,128,256]{2,1,0:T(8,128)S(1)}, u32[]{:S(2)}, u32[]{:S(2)}) collective-permute-start(f32[8,128,256]{2,1,0:T(8,128)S(1)} %get-tuple-element.40.own_ref), channel_id=1, source_target_pairs={{0,1},{1,0},{2,3},{3,2},{4,5},{5,4},{6,7},{7,6},{8,9},{9,8},{10,11... | collective-permute-start | bytes 3145736 | tf_op jit(solution)/shard_map/ppermute | solution.py:363
  10.4 16.0 %collective-permute-start.1 = (f32[128,256]{1,0:T(8,128)S(1)}, f32[128,256]{1,0:T(8,128)S(1)}, u32[]{:S(2)}, u32[]{:S(2)}) collective-permute-start(f32[128,256]{1,0:T(8,128)S(1)} %get-tuple-element.47), channel_id=1, source_target_pairs={{0,2},{1,15},{2,4},{3,1},{4,6},{5,3},{6,8},{7,5},{8,10},{9,7},{10,... | collective-permute-start | bytes 393224 | tf_op jit(solution)/shard_map/ppermute | solution.py:363
  14.3 12.1 %collective-permute-start.2 = (f32[128,256]{1,0:T(8,128)S(1)}, f32[128,256]{1,0:T(8,128)S(1)}, u32[]{:S(2)}, u32[]{:S(2)}) collective-permute-start(f32[128,256]{1,0:T(8,128)S(1)} %get-tuple-element.48), channel_id=1, source_target_pairs={{0,4},{1,13},{2,6},{3,15},{4,8},{5,1},{6,10},{7,3},{8,12},{9,5},{1... | collective-permute-start | bytes 393224 | tf_op jit(solution)/shard_map/ppermute | solution.py:363
  15.5 10.9 %collective-permute-start.3 = (f32[128,256]{1,0:T(8,128)S(1)}, f32[128,256]{1,0:T(8,128)S(1)}, u32[]{:S(2)}, u32[]{:S(2)}) collective-permute-start(f32[128,256]{1,0:T(8,128)S(1)} %get-tuple-element.49), channel_id=1, source_target_pairs={{0,6},{1,11},{2,8},{3,13},{4,10},{5,15},{6,12},{7,1},{8,14},{9,3},... | collective-permute-start | bytes 393224 | tf_op jit(solution)/shard_map/ppermute | solution.py:363
  15.9 10.5 %collective-permute-start.4 = (f32[128,128]{1,0:T(8,128)S(1)}, f32[128,128]{1,0:T(8,128)S(1)}, u32[]{:S(2)}, u32[]{:S(2)}) collective-permute-start(f32[128,128]{1,0:T(8,128)S(1)} %get-tuple-element.50), channel_id=1, source_target_pairs={{0,8},{1,9},{2,10},{3,11},{4,12},{5,13},{6,14},{7,15},{8,0},{9,1},... | collective-permute-start | bytes 196616 | tf_op jit(solution)/shard_map/ppermute | solution.py:363
  21.8 26.8 %all-to-all-start = ((f32[8,136,128]{2,1,0:T(8,128)}), f32[8,136,128]{2,1,0:T(8,128)S(1)}, u32[]{:S(2)}, u32[]{:S(2)}) async-start(f32[8,136,128]{2,1,0:T(8,128)} %get-tuple-element.64), calls=%async_computation | async-start | bytes 1114112 | tf_op jit(solution)/shard_map/all_to_all | solution.py:374
  26.4 4.3 %collective-permute-start.5 = (f32[128,256]{1,0:T(8,128)S(1)}, f32[128,256]{1,0:T(8,128)S(1)}, u32[]{:S(2)}, u32[]{:S(2)}) collective-permute-start(f32[128,256]{1,0:T(8,128)S(1)} %collective-permute-done.1.y1_ref), channel_id=1, source_target_pairs={{0,1},{1,0},{2,3},{3,2},{4,5},{5,4},{6,7},{7,6},{8,9},{9,8},{10,11... | collective-permute-start | bytes 393224 | tf_op jit(solution)/shard_map/ppermute | solution.py:363
  28.9 1.8 %collective-permute-start.6 = (f32[128,256]{1,0:T(8,128)S(1)}, f32[128,256]{1,0:T(8,128)S(1)}, u32[]{:S(2)}, u32[]{:S(2)}) collective-permute-start(f32[128,256]{1,0:T(8,128)S(1)} %collective-permute-done.2.y2_ref), channel_id=1, source_target_pairs={{0,1},{1,0},{2,3},{3,2},{4,5},{5,4},{6,7},{7,6},{8,9},{9,8},{10,11... | collective-permute-start | bytes 393224 | tf_op jit(solution)/shard_map/ppermute | solution.py:363
  29.0 1.8 %collective-permute-start.7 = (f32[128,256]{1,0:T(8,128)S(1)}, f32[128,256]{1,0:T(8,128)S(1)}, u32[]{:S(2)}, u32[]{:S(2)}) collective-permute-start(f32[128,256]{1,0:T(8,128)S(1)} %collective-permute-done.3.y3_ref), channel_id=1, source_target_pairs={{0,1},{1,0},{2,3},{3,2},{4,5},{5,4},{6,7},{7,6},{8,9},{9,8},{10,11... | collective-permute-start | bytes 393224 | tf_op jit(solution)/shard_map/ppermute | solution.py:363
  29.5 1.3 %collective-permute-start.8 = (f32[128,128]{1,0:T(8,128)S(1)}, f32[128,128]{1,0:T(8,128)S(1)}, u32[]{:S(2)}, u32[]{:S(2)}) collective-permute-start(f32[128,128]{1,0:T(8,128)S(1)} %collective-permute-done.4.y4_ref), channel_id=1, source_target_pairs={{0,1},{1,0},{2,3},{3,2},{4,5},{5,4},{6,7},{7,6},{8,9},{9,8},{10,11... | collective-permute-start | bytes 196616 | tf_op jit(solution)/shard_map/ppermute | solution.py:363
  31.5 6.1 %collective-permute-start.9 = (f32[128,256]{1,0:T(8,128)S(1)}, f32[128,256]{1,0:T(8,128)S(1)}, u32[]{:S(2)}, u32[]{:S(2)}) collective-permute-start(f32[128,256]{1,0:T(8,128)S(1)} %get-tuple-element.60.own_ref), channel_id=1, source_target_pairs={{0,16},{1,49},{2,18},{3,51},{4,20},{5,53},{6,22},{7,55},{8,24},{9,... | collective-permute-start | bytes 393224 | tf_op jit(solution)/shard_map/ppermute | solution.py:363
  34.2 5.6 %collective-permute-start.10 = (f32[128,128]{1,0:T(8,128)S(1)}, f32[128,128]{1,0:T(8,128)S(1)}, u32[]{:S(2)}, u32[]{:S(2)}) collective-permute-start(f32[128,128]{1,0:T(8,128)S(1)} %get-tuple-element.61), channel_id=1, source_target_pairs={{0,32},{1,33},{2,34},{3,35},{4,36},{5,37},{6,38},{7,39},{8,40},{9,... | collective-permute-start | bytes 196616 | tf_op jit(solution)/shard_map/ppermute | solution.py:363
  37.6 3.9 %collective-permute-start.11 = (f32[128,256]{1,0:T(8,128)S(1)}, f32[128,256]{1,0:T(8,128)S(1)}, u32[]{:S(2)}, u32[]{:S(2)}) collective-permute-start(f32[128,256]{1,0:T(8,128)S(1)} %collective-permute-done.9.y1_ref), channel_id=1, source_target_pairs={{0,1},{1,0},{2,3},{3,2},{4,5},{5,4},{6,7},{7,6},{8,9},{9,8},{10,11... | collective-permute-start | bytes 393224 | tf_op jit(solution)/shard_map/ppermute | solution.py:363
  39.9 1.5 %collective-permute-start.12 = (f32[128,128]{1,0:T(8,128)S(1)}, f32[128,128]{1,0:T(8,128)S(1)}, u32[]{:S(2)}, u32[]{:S(2)}) collective-permute-start(f32[128,128]{1,0:T(8,128)S(1)} %collective-permute-done.10.y2_ref), channel_id=1, source_target_pairs={{0,1},{1,0},{2,3},{3,2},{4,5},{5,4},{6,7},{7,6},{8,9},{9,8},{10,11... | collective-permute-start | bytes 196616 | tf_op jit(solution)/shard_map/ppermute | solution.py:363
  41.9 6.1 %collective-permute-start.13 = (f32[128,256]{1,0:T(8,128)S(1)}, f32[128,256]{1,0:T(8,128)S(1)}, u32[]{:S(2)}, u32[]{:S(2)}) collective-permute-start(f32[128,256]{1,0:T(8,128)S(1)} %get-tuple-element.62.own_ref), channel_id=1, source_target_pairs={{0,64},{1,193},{2,66},{3,195},{4,68},{5,197},{6,70},{7,199},{8,72}... | collective-permute-start | bytes 393224 | tf_op jit(solution)/shard_map/ppermute | solution.py:363
  44.7 5.6 %collective-permute-start.14 = (f32[128,128]{1,0:T(8,128)S(1)}, f32[128,128]{1,0:T(8,128)S(1)}, u32[]{:S(2)}, u32[]{:S(2)}) collective-permute-start(f32[128,128]{1,0:T(8,128)S(1)} %get-tuple-element.63), channel_id=1, source_target_pairs={{0,128},{1,129},{2,130},{3,131},{4,132},{5,133},{6,134},{7,135},{8... | collective-permute-start | bytes 196616 | tf_op jit(solution)/shard_map/ppermute | solution.py:363
  48.1 3.1 %collective-permute-start.15 = (f32[128,256]{1,0:T(8,128)S(1)}, f32[128,256]{1,0:T(8,128)S(1)}, u32[]{:S(2)}, u32[]{:S(2)}) collective-permute-start(f32[128,256]{1,0:T(8,128)S(1)} %collective-permute-done.13.y1_ref), channel_id=1, source_target_pairs={{0,1},{1,0},{2,3},{3,2},{4,5},{5,4},{6,7},{7,6},{8,9},{9,8},{10,11... | collective-permute-start | bytes 393224 | tf_op jit(solution)/shard_map/ppermute | solution.py:363
  50.3 1.7 %collective-permute-start.16 = (f32[128,128]{1,0:T(8,128)S(1)}, f32[128,128]{1,0:T(8,128)S(1)}, u32[]{:S(2)}, u32[]{:S(2)}) collective-permute-start(f32[128,128]{1,0:T(8,128)S(1)} %collective-permute-done.14.y2_ref), channel_id=1, source_target_pairs={{0,1},{1,0},{2,3},{3,2},{4,5},{5,4},{6,7},{7,6},{8,9},{9,8},{10,11... | collective-permute-start | bytes 196616 | tf_op jit(solution)/shard_map/ppermute | solution.py:363
